TPU v7x, 32 devices: a whole 2x2x4 slice. The times are simulated.
32 devices in a mesh: patch: 8 (over z, x), lat: 4 (over y, core).
Axes of the slice: x: 2, y: 2, z: 4, core: 2. Of those that a mesh axis runs over, the one named last changes fastest.
Arguments:
- obs_values: bfloat16 [4096, 96], P(('patch', 'lat')), may hold values from -6 to 6
- obs_count: int32 [32, 32], P(('patch', 'lat')), may hold values from 0 to 4, as said below
- obs_node: int32 [4096, 3], P(('patch', 'lat')), may hold values from 0 to 319
- mesh_init: bfloat16 [10240, 512], P(('patch', 'lat')), may hold values from -6 to 6
- mesh_offset: int32 [10240, 6], P(('patch', 'lat')), may hold values from -128 to 128, as said below
- weights_flat: bfloat16 [32, 75264], P(('patch', 'lat')), may hold values from -0.25 to 0.25
- edge_bias: float32 [2, 512], replicated, may hold values from -3 to 3
- node_bias: float32 [2, 512], replicated, may hold values from -3 to 3
- norm_gain: float32 [2, 512], replicated, may hold values from 0.1 to 1.9
Outputs:
- mesh_latent: bfloat16 [10240, 512], P(('patch', 'lat'))
Inputs may be any that keep to these rules, and one draw needn't show every extreme that they name: obs_count[s, d] counts the live slots (the first ones) among the 4 slots that device s holds for device d; each source fills all 4 slots for some destination, and some destination receives 4 live slots from every source. `obs_node`: local node on the destination device. The k-th incoming edge of node n comes from node (n + mesh_offset[n, k]) mod 10240; offsets of both -128 and 128 occur.
All inputs are finite; a program needn't handle non-finite values.
Results may differ from a plain program's by a relative error of at most 0.0085.
Values may be sent and summed in bfloat16 or wider, within the bound.
No kernel may reach another device: no remote copies, remote signals or barrier semaphores. Data moves between devices by JAX's collectives and lax.ppermute only.
A program may use at most 128 MiB of HBM per device.

v0:
```python
import jax
import jax.numpy as jnp
from jax import lax
from jax.sharding import PartitionSpec as P

D = 512
CH = 96
OBS_EDGES = 3
DEG = 6
HALO = 128


def extended(block, sides, width):
    for axis, dim in sides:
        count = lax.axis_size(axis)
        forward = [(i, i + 1) for i in range(count - 1)]
        forward.append((count - 1, 0))
        backward = [(target, source) for source, target in forward]
        low = lax.ppermute(
            lax.slice_in_dim(block, block.shape[dim] - width, None, axis=dim), axis, forward
        )
        high = lax.ppermute(lax.slice_in_dim(block, 0, width, axis=dim), axis, backward)
        block = jnp.concatenate([low, block, high], axis=dim)
    return block


def unpack(flat):
    shapes = ((CH, D), (D, 2 * D), (D, D), (D, D), (D, 3 * D), (D, D), (D, D))
    pieces = []
    offset = 0
    for height, breadth in shapes:
        pieces.append(flat[offset : offset + height * breadth].reshape(height, breadth))
        offset = offset + height * breadth
    return pieces


def layer_norm(values, gain):
    center = values - jnp.mean(values, axis=-1, keepdims=True)
    spread = jnp.mean(center * center, axis=-1, keepdims=True)
    return center * lax.rsqrt(spread + 1e-05) * gain


def embed_rows(rows, w_in):
    return jnp.dot(rows, w_in, preferred_element_type=jnp.float32).astype(jnp.bfloat16)


def deliver(values, nodes, counts):
    return (
        lax.all_to_all(
            lax.all_to_all(values, "patch", split_axis=0, concat_axis=0, tiled=True),
            "lat",
            split_axis=1,
            concat_axis=1,
            tiled=True,
        ),
        lax.all_to_all(
            lax.all_to_all(nodes, "patch", split_axis=0, concat_axis=0, tiled=True),
            "lat",
            split_axis=1,
            concat_axis=1,
            tiled=True,
        ),
        lax.all_to_all(
            lax.all_to_all(counts, "patch", split_axis=0, concat_axis=0, tiled=True),
            "lat",
            split_axis=1,
            concat_axis=1,
            tiled=True,
        ),
    )


def shards(
    obs_values,
    obs_count,
    obs_node,
    mesh_init,
    mesh_offset,
    weights_flat,
    edge_bias,
    node_bias,
    norm_gain,
):
    n_patch = lax.axis_size("patch")
    n_lat = lax.axis_size("lat")
    senders = n_patch * n_lat
    capacity = obs_values.shape[0] // senders
    node_dev = mesh_init.shape[0]
    table = lax.all_gather(weights_flat, ("patch", "lat"), axis=0, tiled=True)
    w_in, w_enc, w_agg, w_out, w_proc, w_pagg, w_pout = unpack(table.reshape(-1))
    breadth = obs_values.shape[1]
    arrived, targets, counts = deliver(
        obs_values.reshape(n_patch, n_lat, capacity, breadth),
        obs_node.reshape(n_patch, n_lat, capacity, OBS_EDGES),
        obs_count.reshape(n_patch, n_lat),
    )
    arrived = arrived.reshape(senders * capacity, breadth)
    targets = targets.reshape(senders * capacity, OBS_EDGES)
    embedded = embed_rows(arrived, w_in)
    alive = (
        (jnp.arange(capacity, dtype=jnp.int32)[None, :] < counts.reshape(senders, 1))
        .astype(jnp.float32)
        .reshape(-1)
    )
    encoded = jnp.dot(mesh_init, w_enc, preferred_element_type=jnp.float32)
    query = encoded[:, :D] + edge_bias[0]
    total_rows = senders * capacity
    block = min(512, total_rows)
    turns = total_rows // block
    node_ids = jnp.arange(node_dev, dtype=jnp.int32)[None, :]

    def encode_block(block_index, totals):
        start = block_index * block
        piece = lax.dynamic_slice_in_dim(embedded, start, block, 0).astype(jnp.float32)
        nodes = lax.dynamic_slice_in_dim(targets, start, block, 0)
        weight = lax.dynamic_slice_in_dim(alive, start, block, 0)[:, None]
        for which in range(OBS_EDGES):
            selector = (nodes[:, which][:, None] == node_ids).astype(jnp.float32)
            picked = jnp.dot(selector, query, precision=lax.Precision.HIGHEST)
            message = jax.nn.silu(piece + picked) * weight
            totals = totals + lax.dot_general(
                selector, message, (((0,), (0,)), ((), ())), precision=lax.Precision.HIGHEST
            )
        return totals

    totals = lax.fori_loop(0, turns, encode_block, jnp.zeros((node_dev, D), jnp.float32))
    gathered = totals.astype(jnp.bfloat16)
    hidden = jax.nn.silu(
        encoded[:, D:] + jnp.dot(gathered, w_agg, preferred_element_type=jnp.float32) + node_bias[0]
    ).astype(jnp.bfloat16)
    first = (
        mesh_init.astype(jnp.float32)
        + layer_norm(jnp.dot(hidden, w_out, preferred_element_type=jnp.float32), norm_gain[0])
    ).astype(jnp.bfloat16)
    projected = jnp.dot(first, w_proc, preferred_element_type=jnp.float32)
    sources = projected[:, :D].astype(jnp.bfloat16)
    target = projected[:, D : 2 * D] + edge_bias[1]
    padded = extended(sources, ((("patch", "lat"), 0),), HALO)
    local_ids = jnp.arange(node_dev, dtype=jnp.int32) + HALO
    pooled = jnp.zeros((node_dev, D), jnp.float32)
    for which in range(DEG):
        anchor = local_ids + mesh_offset[:, which]
        pooled = pooled + jax.nn.silu(jnp.take(padded, anchor, axis=0).astype(jnp.float32) + target)
    hidden2 = jax.nn.silu(
        projected[:, 2 * D :]
        + jnp.dot(pooled.astype(jnp.bfloat16), w_pagg, preferred_element_type=jnp.float32)
        + node_bias[1]
    ).astype(jnp.bfloat16)
    return (
        first.astype(jnp.float32)
        + layer_norm(jnp.dot(hidden2, w_pout, preferred_element_type=jnp.float32), norm_gain[1])
    ).astype(jnp.bfloat16)


def solution(mesh):
    return jax.shard_map(
        shards,
        mesh=mesh,
        in_specs=(
            P(("patch", "lat"), None),
            P(("patch", "lat"), None),
            P(("patch", "lat"), None),
            P(("patch", "lat"), None),
            P(("patch", "lat"), None),
            P(("patch", "lat"), None),
            P(),
            P(),
            P(),
        ),
        out_specs=P(("patch", "lat"), None),
        check_vma=False,
    )
```

profile of v0, /device:TPU:0, one launch (start us, length us, event | category | flops | bytes accessed | tf_op | source)
XLA Modules:
  0.0 260.3 jit_solution(6021291949161695831)
XLA Ops:
  7.8 1.3 reduce.18
  9.8 7.3 %all-to-all-start.4 = ((s32[8,1,4]{2,1,0:T(1,128)}), s32[8,1,4]{2,1,0:T(1,128)S(1)}, u32[]{:S(2)}, u32[]{:S(2)}) async-start(s32[8,1,4]{2,1,0:T(1,128)} %bitcast.5), calls=%async_computation.4 | async-start | bytes 8192 | tf_op jit(solution)/shard_map/all_to_all | solution.py:64
  23.5 5.9 %all-to-all-start = ((s32[8,4,4,3]{2,1,3,0:T(4,128)}), s32[8,4,4,3]{2,1,3,0:T(4,128)S(1)}, u32[]{:S(2)}, u32[]{:S(2)}) async-start(s32[8,4,4,3]{2,1,3,0:T(4,128)} %copy.15), calls=%async_computation | async-start | bytes 98304 | tf_op jit(solution)/shard_map/all_to_all | solution.py:57
  30.1 6.2 %all-to-all-done = s32[8,4,4,3]{2,1,3,0:T(4,128)S(1)} async-done(((s32[8,4,4,3]{2,1,3,0:T(4,128)}), s32[8,4,4,3]{2,1,3,0:T(4,128)S(1)}, u32[]{:S(2)}, u32[]{:S(2)}) %all-to-all-start) | async-done | bytes 1568 | tf_op jit(solution)/shard_map/all_to_all | solution.py:57
  36.3 3.2 %all-to-all-start.5 = ((s32[8,4,1]{0,2,1:T(1,128)}), s32[8,4,1]{0,2,1:T(1,128)S(1)}, u32[]{:S(2)}, u32[]{:S(2)}) async-start(s32[8,4,1]{0,2,1:T(1,128)} %copy.23), calls=%async_computation.5 | async-start | bytes 4096 | tf_op jit(solution)/shard_map/all_to_all | solution.py:63
  40.3 3.0 %all-to-all-done.5 = s32[8,4,1]{0,2,1:T(1,128)S(1)} async-done(((s32[8,4,1]{0,2,1:T(1,128)}), s32[8,4,1]{0,2,1:T(1,128)S(1)}, u32[]{:S(2)}, u32[]{:S(2)}) %all-to-all-start.5) | async-done | bytes 160 | tf_op jit(solution)/shard_map/all_to_all | solution.py:63
  43.3 3.3 %all-to-all-start.1 = ((s32[8,4,4,3]{0,2,3,1:T(4,128)}), s32[8,4,4,3]{0,2,3,1:T(4,128)S(1)}, u32[]{:S(2)}, u32[]{:S(2)}) async-start(s32[8,4,4,3]{0,2,3,1:T(4,128)} %copy.16), calls=%async_computation.1 | async-start | bytes 49152 | tf_op jit(solution)/shard_map/all_to_all | solution.py:56
  46.5 1.5 copy.18
  48.2 2.2 all-to-all-done.1
  50.4 3.3 %all-to-all-start.2 = ((bf16[8,4,4,96]{3,2,1,0:T(4,128)(2,1)}), bf16[8,4,4,96]{3,2,1,0:T(4,128)(2,1)S(1)}, u32[]{:S(2)}, u32[]{:S(2)}) async-start(bf16[8,4,4,96]{3,2,1,0:T(4,128)(2,1)} %bitcast.2), calls=%async_computation.2 | async-start | bytes 65536 | tf_op jit(solution)/shard_map/all_to_all | solution.py:50
  54.2 6.2 %all-to-all-done.2 = bf16[8,4,4,96]{3,2,1,0:T(4,128)(2,1)S(1)} async-done(((bf16[8,4,4,96]{3,2,1,0:T(4,128)(2,1)}), bf16[8,4,4,96]{3,2,1,0:T(4,128)(2,1)S(1)}, u32[]{:S(2)}, u32[]{:S(2)}) %all-to-all-start.2) | async-done | bytes 24608 | tf_op jit(solution)/shard_map/all_to_all | solution.py:50
  61.0 3.3 %all-to-all-start.3 = ((bf16[8,4,4,96]{3,2,0,1:T(4,128)(2,1)}), bf16[8,4,4,96]{3,2,0,1:T(4,128)(2,1)S(1)}, u32[]{:S(2)}, u32[]{:S(2)}) async-start(bf16[8,4,4,96]{3,2,0,1:T(4,128)(2,1)} %copy.19), calls=%async_computation.3 | async-start | bytes 65536 | tf_op jit(solution)/shard_map/all_to_all | solution.py:49
  64.3 4.3 %all-to-all-done.3 = bf16[8,4,4,96]{3,2,0,1:T(4,128)(2,1)S(1)} async-done(((bf16[8,4,4,96]{3,2,0,1:T(4,128)(2,1)}), bf16[8,4,4,96]{3,2,0,1:T(4,128)(2,1)S(1)}, u32[]{:S(2)}, u32[]{:S(2)}) %all-to-all-start.3) | async-done | bytes 24608 | tf_op jit(solution)/shard_map/all_to_all | solution.py:49
  68.6 27.7 %all-gather.3.cloned.1.call-done = bf16[32,1,75264]{2,1,0:T(2,128)(2,1)} async-done(((bf16[1,1,75264]{2,1,0:T(2,128)(2,1)}), bf16[32,1,75264]{2,1,0:T(2,128)(2,1)}) %all-gather.3.cloned.1.call-update) | async-done | bytes 4816912 | tf_op jit(solution)/shard_map/all_gather | solution.py:89
  96.3 87.6 %reduce = bf16[32,75264]{1,0:T(8,128)(2,1)} reduce(bf16[32,1,75264]{2,1,0:T(2,128)(2,1)} %all-gather.3.cloned.1.call-done, bf16[]{:T(256)} %constant.49), dimensions={1}, to_apply=%all-gather.reduce_sub_computation | reduce | bytes 9633794 | tf_op jit(solution)/shard_map/all_gather | solution.py:89
  183.9 9.6 %slice.107 = bf16[4704,512]{1,0:T(8,128)(2,1)} reshape(bf16[32,75264]{1,0:T(8,128)(2,1)} %reduce) | data formatting | bytes 9633792 | tf_op jit(solution)/shard_map/slice | solution.py:32
  193.5 10.3 %slice.103 = bf16[2352,1024]{1,0:T(8,128)(2,1)} reshape(bf16[32,75264]{1,0:T(8,128)(2,1)} %reduce) | data formatting | bytes 9633792 | tf_op jit(solution)/shard_map/slice | solution.py:32
  203.8 9.7 %reshape.98 = bf16[2408448]{0:T(1024)(128)(2,1)} reshape(bf16[32,75264]{1,0:T(8,128)(2,1)} %reduce) | data formatting | bytes 9633792 | tf_op jit(solution)/shard_map/reshape | solution.py:90
  214.6 1.7 fusion.4
  219.5 2.0 fusion.80
  223.1 1.8 reshape.99
  224.9 1.3 add_convert_fusion.2
  226.2 2.0 fusion.83
  228.5 5.1 %collective-permute-start.1 = (bf16[128,512]{1,0:T(8,128)(2,1)S(1)}, bf16[128,512]{1,0:T(8,128)(2,1)S(1)}, u32[]{:S(2)}, u32[]{:S(2)}) collective-permute-start(bf16[128,512]{1,0:T(8,128)(2,1)S(1)} %get-tuple-element.37), channel_id=1, source_target_pairs={{1,0},{2,1},{3,2},{4,3},{5,4},{6,5},{7,6},{8,7},{9,8},{10,9},{11,1... | collective-permute-start | bytes 393224 | tf_op jit(solution)/shard_map/ppermute | solution.py:22
  233.7 2.6 collective-permute-done
  236.3 2.2 gather_fusion.4
  238.6 2.0 gather_fusion
  240.6 2.0 gather_fusion.1
  242.6 2.0 gather_fusion.2
  244.7 2.0 gather_fusion.3
  246.7 2.0 gather_fusion.5
  248.7 3.5 %fusion.84 = (f32[320]{0:T(512)S(1)}, f32[320,512]{1,0:T(8,128)S(1)}) fusion(bf16[4704,512]{1,0:T(8,128)(2,1)} %slice.107, f32[320,1536]{1,0:T(8,128)} %get-tuple-element.50, f32[512]{0:T(512)S(1)} %bitcast.37, bf16[320,512]{1,0:T(8,128)(2,1)S(1)} %gather_fusion.5, bf16[320,512]{1,0:T(8,128)(2,1)S(1)} %gather_fusion.4, ...), kind=kOutput, calls=%fused_computation.131 | convolution fusion | flops 344882880 | bytes 4988992 | tf_op jit(solution)/shard_map/dot_general | solution.py:151
  (59 shorter events, 18.4 us)
Async XLA Ops:
  6.5 89.8 %all-gather.3.cloned.1.call-start = ((), (), s32[]{:S(2)}) async-start(), calls=%async_computation.6 | async-start | bytes 9934848 | tf_op jit(solution)/shard_map/all_gather | solution.py:89
  9.8 13.8 %all-to-all-start.4 = ((s32[8,1,4]{2,1,0:T(1,128)}), s32[8,1,4]{2,1,0:T(1,128)S(1)}, u32[]{:S(2)}, u32[]{:S(2)}) async-start(s32[8,1,4]{2,1,0:T(1,128)} %bitcast.5), calls=%async_computation.4 | async-start | bytes 8192 | tf_op jit(solution)/shard_map/all_to_all | solution.py:64
  23.5 12.8 %all-to-all-start = ((s32[8,4,4,3]{2,1,3,0:T(4,128)}), s32[8,4,4,3]{2,1,3,0:T(4,128)S(1)}, u32[]{:S(2)}, u32[]{:S(2)}) async-start(s32[8,4,4,3]{2,1,3,0:T(4,128)} %copy.15), calls=%async_computation | async-start | bytes 98304 | tf_op jit(solution)/shard_map/all_to_all | solution.py:57
  36.3 7.0 %all-to-all-start.5 = ((s32[8,4,1]{0,2,1:T(1,128)}), s32[8,4,1]{0,2,1:T(1,128)S(1)}, u32[]{:S(2)}, u32[]{:S(2)}) async-start(s32[8,4,1]{0,2,1:T(1,128)} %copy.23), calls=%async_computation.5 | async-start | bytes 4096 | tf_op jit(solution)/shard_map/all_to_all | solution.py:63
  43.3 7.1 %all-to-all-start.1 = ((s32[8,4,4,3]{0,2,3,1:T(4,128)}), s32[8,4,4,3]{0,2,3,1:T(4,128)S(1)}, u32[]{:S(2)}, u32[]{:S(2)}) async-start(s32[8,4,4,3]{0,2,3,1:T(4,128)} %copy.16), calls=%async_computation.1 | async-start | bytes 49152 | tf_op jit(solution)/shard_map/all_to_all | solution.py:56
  50.4 10.0 %all-to-all-start.2 = ((bf16[8,4,4,96]{3,2,1,0:T(4,128)(2,1)}), bf16[8,4,4,96]{3,2,1,0:T(4,128)(2,1)S(1)}, u32[]{:S(2)}, u32[]{:S(2)}) async-start(bf16[8,4,4,96]{3,2,1,0:T(4,128)(2,1)} %bitcast.2), calls=%async_computation.2 | async-start | bytes 65536 | tf_op jit(solution)/shard_map/all_to_all | solution.py:50
  61.0 7.6 %all-to-all-start.3 = ((bf16[8,4,4,96]{3,2,0,1:T(4,128)(2,1)}), bf16[8,4,4,96]{3,2,0,1:T(4,128)(2,1)S(1)}, u32[]{:S(2)}, u32[]{:S(2)}) async-start(bf16[8,4,4,96]{3,2,0,1:T(4,128)(2,1)} %copy.19), calls=%async_computation.3 | async-start | bytes 65536 | tf_op jit(solution)/shard_map/all_to_all | solution.py:49
  203.8 10.8 %copy-start.1 = (bf16[320,512]{1,0:T(8,128)(2,1)S(1)}, bf16[320,512]{1,0:T(8,128)(2,1)}, u32[]{:S(2)}) copy-start(bf16[320,512]{1,0:T(8,128)(2,1)} %param.14) | copy-start | bytes 983044
  221.5 0.8 copy-start
  221.5 1.6 slice-start
  228.2 8.0 %collective-permute-start = (bf16[128,512]{1,0:T(8,128)(2,1)S(1)}, bf16[128,512]{1,0:T(8,128)(2,1)S(1)}, u32[]{:S(2)}, u32[]{:S(2)}) collective-permute-start(bf16[128,512]{1,0:T(8,128)(2,1)S(1)} %get-tuple-element.36), channel_id=1, source_target_pairs={{0,1},{1,2},{2,3},{3,4},{4,5},{5,6},{6,7},{7,8},{8,9},{9,10},{10,1... | collective-permute-start | bytes 393224 | tf_op jit(solution)/shard_map/ppermute | solution.py:19
  228.5 7.7 %collective-permute-start.1 = (bf16[128,512]{1,0:T(8,128)(2,1)S(1)}, bf16[128,512]{1,0:T(8,128)(2,1)S(1)}, u32[]{:S(2)}, u32[]{:S(2)}) collective-permute-start(bf16[128,512]{1,0:T(8,128)(2,1)S(1)} %get-tuple-element.37), channel_id=1, source_target_pairs={{1,0},{2,1},{3,2},{4,3},{5,4},{6,5},{7,6},{8,7},{9,8},{10,9},{11,1... | collective-permute-start | bytes 393224 | tf_op jit(solution)/shard_map/ppermute | solution.py:22
Sparse Core Ops, SparseCore 0:
  10.2 86.1 all-gather.2
where the time goes:
time: 261 us; the launch traced here: 260 us
  other arithmetic  93.5 us (36%)
  local copies, waits for them, and re-layouts  55.1 us (21%)
  waiting for transfers between devices  53 us (20%)
  starting transfers between devices  31.7 us (12%)
  between operations  13.7 us (5%)
  matrix products  13.4 us (5%)
    all_gather x1, other arithmetic, shards(): table = lax.all_gather(weights_flat, ('patch', 'lat'), axis=0, tiled=True)  87.6 us
    all_gather x1, waiting for transfers between devices, shards(): table = lax.all_gather(weights_flat, ('patch', 'lat'), axis=0, tiled=True)  27.7 us
    slice x4, local copies, waits for them, and re-layouts, unpack(): flat[offset:offset + height * breadth].reshape(height, breadth)  20.7 us
    gather x6, local copies, waits for them, and re-layouts, shards(): jnp.take(padded, anchor, axis=0).astype(jnp.float32) + target  12.4 us
    reshape x1, local copies, waits for them, and re-layouts, shards(): table.reshape(-1)  9.71 us
    all_to_all x1, starting transfers between devices, deliver(): lax.all_to_all(counts, 'patch', split_axis=0, concat_axis=0, tiled=True)  7.28 us
    all_to_all x1, waiting for transfers between devices, deliver(): lax.all_to_all(nodes, 'patch', split_axis=0, concat_axis=0, tiled=True)  6.21 us
    all_to_all x1, waiting for transfers between devices, deliver(): lax.all_to_all(values, 'patch', split_axis=0, concat_axis=0, tiled=True)  6.17 us
  transfers between devices with their start and end apart: 9, of which 8 were waited for; matrix products, arithmetic and copies ran while one was open for 5% of the time, Pallas kernels for 0%

commit v1 on v0

--- a/solution.py
+++ b/solution.py
@@ -8,6 +8,13 @@
 OBS_EDGES = 3
 DEG = 6
 HALO = 128
+
+
+def stacked_exchange(shard, axis, split, join):
+    n_dev = lax.axis_size(axis)
+    blocks = jnp.stack(jnp.split(shard, n_dev, axis=split), axis=0)
+    blocks = lax.all_to_all(blocks, axis, split_axis=0, concat_axis=0)
+    return jnp.concatenate(blocks, axis=join)
 
 
 def extended(block, sides, width):
@@ -46,12 +53,8 @@
 
 def deliver(values, nodes, counts):
     return (
-        lax.all_to_all(
-            lax.all_to_all(values, "patch", split_axis=0, concat_axis=0, tiled=True),
-            "lat",
-            split_axis=1,
-            concat_axis=1,
-            tiled=True,
+        stacked_exchange(
+            lax.all_to_all(values, "patch", split_axis=0, concat_axis=0, tiled=True), "lat", 1, 1
         ),
         lax.all_to_all(
             lax.all_to_all(nodes, "patch", split_axis=0, concat_axis=0, tiled=True),

time: 261 us -> 261 us (level)
  no operation moved by 1% of the time
where the time goes in v1:
time: 261 us; the launch traced here: 260 us
  other arithmetic  94.1 us (36%)
  local copies, waits for them, and re-layouts  54.5 us (21%)
  waiting for transfers between devices  53 us (20%)
  starting transfers between devices  31.7 us (12%)
  between operations  13.7 us (5%)
  matrix products  13.4 us (5%)
    all_gather x1, other arithmetic, shards(): table = lax.all_gather(weights_flat, ('patch', 'lat'), axis=0, tiled=True)  87.6 us
    all_gather x1, waiting for transfers between devices, shards(): table = lax.all_gather(weights_flat, ('patch', 'lat'), axis=0, tiled=True)  27.9 us
    slice x4, local copies, waits for them, and re-layouts, unpack(): flat[offset:offset + height * breadth].reshape(height, breadth)  20.7 us
    gather x6, local copies, waits for them, and re-layouts, shards(): jnp.take(padded, anchor, axis=0).astype(jnp.float32) + target  12.4 us
    reshape x1, local copies, waits for them, and re-layouts, shards(): table.reshape(-1)  9.73 us
    all_to_all x1, starting transfers between devices, deliver(): lax.all_to_all(counts, 'patch', split_axis=0, concat_axis=0, tiled=True)  7.28 us
    all_to_all x1, waiting for transfers between devices, deliver(): lax.all_to_all(nodes, 'patch', split_axis=0, concat_axis=0, tiled=True)  6.17 us
    all_to_all x1, waiting for transfers between devices, deliver(): lax.all_to_all(values, 'patch', split_axis=0, concat_axis=0, tiled=True)  6.17 us
  transfers between devices with their start and end apart: 9, of which 8 were waited for; matrix products, arithmetic and copies ran while one was open for 5% of the time, Pallas kernels for 0%

profile of v1, /device:TPU:0, one launch (start us, length us, event | category | flops | bytes accessed | tf_op | source)
XLA Modules:
  0.0 260.4 jit_solution(8363554263484191776)
XLA Ops:
  7.8 1.3 reduce.18
  9.8 7.3 %all-to-all-start.4 = ((s32[8,1,4]{2,1,0:T(1,128)}), s32[8,1,4]{2,1,0:T(1,128)S(1)}, u32[]{:S(2)}, u32[]{:S(2)}) async-start(s32[8,1,4]{2,1,0:T(1,128)} %bitcast.10), calls=%async_computation.4 | async-start | bytes 8192 | tf_op jit(solution)/shard_map/all_to_all | solution.py:67
  23.5 5.9 %all-to-all-start = ((s32[8,4,4,3]{2,1,3,0:T(4,128)}), s32[8,4,4,3]{2,1,3,0:T(4,128)S(1)}, u32[]{:S(2)}, u32[]{:S(2)}) async-start(s32[8,4,4,3]{2,1,3,0:T(4,128)} %copy.23), calls=%async_computation | async-start | bytes 98304 | tf_op jit(solution)/shard_map/all_to_all | solution.py:60
  30.1 6.2 %all-to-all-done = s32[8,4,4,3]{2,1,3,0:T(4,128)S(1)} async-done(((s32[8,4,4,3]{2,1,3,0:T(4,128)}), s32[8,4,4,3]{2,1,3,0:T(4,128)S(1)}, u32[]{:S(2)}, u32[]{:S(2)}) %all-to-all-start) | async-done | bytes 1568 | tf_op jit(solution)/shard_map/all_to_all | solution.py:60
  36.3 3.2 %all-to-all-start.5 = ((s32[8,4,1]{0,2,1:T(1,128)}), s32[8,4,1]{0,2,1:T(1,128)S(1)}, u32[]{:S(2)}, u32[]{:S(2)}) async-start(s32[8,4,1]{0,2,1:T(1,128)} %copy.34), calls=%async_computation.5 | async-start | bytes 4096 | tf_op jit(solution)/shard_map/all_to_all | solution.py:66
  40.3 2.9 %all-to-all-done.5 = s32[8,4,1]{0,2,1:T(1,128)S(1)} async-done(((s32[8,4,1]{0,2,1:T(1,128)}), s32[8,4,1]{0,2,1:T(1,128)S(1)}, u32[]{:S(2)}, u32[]{:S(2)}) %all-to-all-start.5) | async-done | bytes 160 | tf_op jit(solution)/shard_map/all_to_all | solution.py:66
  43.2 3.3 %all-to-all-start.1 = ((s32[8,4,4,3]{0,2,3,1:T(4,128)}), s32[8,4,4,3]{0,2,3,1:T(4,128)S(1)}, u32[]{:S(2)}, u32[]{:S(2)}) async-start(s32[8,4,4,3]{0,2,3,1:T(4,128)} %copy.24), calls=%async_computation.1 | async-start | bytes 49152 | tf_op jit(solution)/shard_map/all_to_all | solution.py:59
  46.4 1.5 copy.26
  48.1 2.2 all-to-all-done.1
  50.3 3.3 %all-to-all-start.2 = ((bf16[8,4,4,96]{3,2,1,0:T(4,128)(2,1)}), bf16[8,4,4,96]{3,2,1,0:T(4,128)(2,1)S(1)}, u32[]{:S(2)}, u32[]{:S(2)}) async-start(bf16[8,4,4,96]{3,2,1,0:T(4,128)(2,1)} %bitcast.2), calls=%async_computation.2 | async-start | bytes 65536 | tf_op jit(solution)/shard_map/all_to_all | solution.py:57
  54.1 6.2 %all-to-all-done.2 = bf16[8,4,4,96]{3,2,1,0:T(4,128)(2,1)S(1)} async-done(((bf16[8,4,4,96]{3,2,1,0:T(4,128)(2,1)}), bf16[8,4,4,96]{3,2,1,0:T(4,128)(2,1)S(1)}, u32[]{:S(2)}, u32[]{:S(2)}) %all-to-all-start.2) | async-done | bytes 24608 | tf_op jit(solution)/shard_map/all_to_all | solution.py:57
  60.9 3.3 %all-to-all-start.3 = ((bf16[4,8,1,4,96]{4,3,1,2,0:T(4,128)(2,1)}), bf16[4,8,1,4,96]{4,3,1,2,0:T(4,128)(2,1)S(1)}, u32[]{:S(2)}, u32[]{:S(2)}) async-start(bf16[4,8,1,4,96]{4,3,1,2,0:T(4,128)(2,1)} %pad_maximum_fusion.1), calls=%async_computation.3 | async-start | bytes 65536 | tf_op jit(solution)/shard_map/all_to_all | solution.py:16
  64.2 4.3 %all-to-all-done.3 = bf16[4,8,1,4,96]{4,3,1,2,0:T(4,128)(2,1)S(1)} async-done(((bf16[4,8,1,4,96]{4,3,1,2,0:T(4,128)(2,1)}), bf16[4,8,1,4,96]{4,3,1,2,0:T(4,128)(2,1)S(1)}, u32[]{:S(2)}, u32[]{:S(2)}) %all-to-all-start.3) | async-done | bytes 24608 | tf_op jit(solution)/shard_map/all_to_all | solution.py:16
  68.5 27.9 %all-gather.3.cloned.1.call-done = bf16[32,1,75264]{2,1,0:T(2,128)(2,1)} async-done(((bf16[1,1,75264]{2,1,0:T(2,128)(2,1)}), bf16[32,1,75264]{2,1,0:T(2,128)(2,1)}) %all-gather.3.cloned.1.call-update) | async-done | bytes 4816912 | tf_op jit(solution)/shard_map/all_gather | solution.py:92
  96.4 87.6 %reduce = bf16[32,75264]{1,0:T(8,128)(2,1)} reduce(bf16[32,1,75264]{2,1,0:T(2,128)(2,1)} %all-gather.3.cloned.1.call-done, bf16[]{:T(256)} %constant.49), dimensions={1}, to_apply=%all-gather.reduce_sub_computation | reduce | bytes 9633794 | tf_op jit(solution)/shard_map/all_gather | solution.py:92
  184.1 9.6 %slice.107 = bf16[4704,512]{1,0:T(8,128)(2,1)} reshape(bf16[32,75264]{1,0:T(8,128)(2,1)} %reduce) | data formatting | bytes 9633792 | tf_op jit(solution)/shard_map/slice | solution.py:39
  193.7 10.3 %slice.103 = bf16[2352,1024]{1,0:T(8,128)(2,1)} reshape(bf16[32,75264]{1,0:T(8,128)(2,1)} %reduce) | data formatting | bytes 9633792 | tf_op jit(solution)/shard_map/slice | solution.py:39
  204.0 9.7 %reshape.98 = bf16[2408448]{0:T(1024)(128)(2,1)} reshape(bf16[32,75264]{1,0:T(8,128)(2,1)} %reduce) | data formatting | bytes 9633792 | tf_op jit(solution)/shard_map/reshape | solution.py:93
  214.8 1.7 fusion.4
  219.7 2.0 fusion.80
  223.3 1.8 reshape.99
  225.1 1.3 add_convert_fusion.2
  226.4 2.0 fusion.83
  228.7 5.1 %collective-permute-start.1 = (bf16[128,512]{1,0:T(8,128)(2,1)S(1)}, bf16[128,512]{1,0:T(8,128)(2,1)S(1)}, u32[]{:S(2)}, u32[]{:S(2)}) collective-permute-start(bf16[128,512]{1,0:T(8,128)(2,1)S(1)} %get-tuple-element.37), channel_id=1, source_target_pairs={{1,0},{2,1},{3,2},{4,3},{5,4},{6,5},{7,6},{8,7},{9,8},{10,9},{11,1... | collective-permute-start | bytes 393224 | tf_op jit(solution)/shard_map/ppermute | solution.py:29
  233.8 2.6 collective-permute-done
  236.5 2.2 gather_fusion.4
  238.7 2.0 gather_fusion
  240.8 2.0 gather_fusion.1
  242.8 2.0 gather_fusion.2
  244.8 2.0 gather_fusion.3
  246.8 2.0 gather_fusion.5
  248.9 3.5 %fusion.84 = (f32[320]{0:T(512)S(1)}, f32[320,512]{1,0:T(8,128)S(1)}) fusion(bf16[4704,512]{1,0:T(8,128)(2,1)} %slice.107, f32[320,1536]{1,0:T(8,128)} %get-tuple-element.54, f32[512]{0:T(512)S(1)} %bitcast.51, bf16[320,512]{1,0:T(8,128)(2,1)S(1)} %gather_fusion.5, bf16[320,512]{1,0:T(8,128)(2,1)S(1)} %gather_fusion.4, ...), kind=kOutput, calls=%fused_computation.136 | convolution fusion | flops 344882880 | bytes 4988992 | tf_op jit(solution)/shard_map/dot_general | solution.py:154
  (60 shorter events, 18.5 us)
Async XLA Ops:
  6.5 89.9 %all-gather.3.cloned.1.call-start = ((), (), s32[]{:S(2)}) async-start(), calls=%async_computation.6 | async-start | bytes 9934848 | tf_op jit(solution)/shard_map/all_gather | solution.py:92
  9.8 13.8 %all-to-all-start.4 = ((s32[8,1,4]{2,1,0:T(1,128)}), s32[8,1,4]{2,1,0:T(1,128)S(1)}, u32[]{:S(2)}, u32[]{:S(2)}) async-start(s32[8,1,4]{2,1,0:T(1,128)} %bitcast.10), calls=%async_computation.4 | async-start | bytes 8192 | tf_op jit(solution)/shard_map/all_to_all | solution.py:67
  23.5 12.8 %all-to-all-start = ((s32[8,4,4,3]{2,1,3,0:T(4,128)}), s32[8,4,4,3]{2,1,3,0:T(4,128)S(1)}, u32[]{:S(2)}, u32[]{:S(2)}) async-start(s32[8,4,4,3]{2,1,3,0:T(4,128)} %copy.23), calls=%async_computation | async-start | bytes 98304 | tf_op jit(solution)/shard_map/all_to_all | solution.py:60
  36.3 6.8 %all-to-all-start.5 = ((s32[8,4,1]{0,2,1:T(1,128)}), s32[8,4,1]{0,2,1:T(1,128)S(1)}, u32[]{:S(2)}, u32[]{:S(2)}) async-start(s32[8,4,1]{0,2,1:T(1,128)} %copy.34), calls=%async_computation.5 | async-start | bytes 4096 | tf_op jit(solution)/shard_map/all_to_all | solution.py:66
  43.2 7.1 %all-to-all-start.1 = ((s32[8,4,4,3]{0,2,3,1:T(4,128)}), s32[8,4,4,3]{0,2,3,1:T(4,128)S(1)}, u32[]{:S(2)}, u32[]{:S(2)}) async-start(s32[8,4,4,3]{0,2,3,1:T(4,128)} %copy.24), calls=%async_computation.1 | async-start | bytes 49152 | tf_op jit(solution)/shard_map/all_to_all | solution.py:59
  50.3 10.0 %all-to-all-start.2 = ((bf16[8,4,4,96]{3,2,1,0:T(4,128)(2,1)}), bf16[8,4,4,96]{3,2,1,0:T(4,128)(2,1)S(1)}, u32[]{:S(2)}, u32[]{:S(2)}) async-start(bf16[8,4,4,96]{3,2,1,0:T(4,128)(2,1)} %bitcast.2), calls=%async_computation.2 | async-start | bytes 65536 | tf_op jit(solution)/shard_map/all_to_all | solution.py:57
  60.9 7.6 %all-to-all-start.3 = ((bf16[4,8,1,4,96]{4,3,1,2,0:T(4,128)(2,1)}), bf16[4,8,1,4,96]{4,3,1,2,0:T(4,128)(2,1)S(1)}, u32[]{:S(2)}, u32[]{:S(2)}) async-start(bf16[4,8,1,4,96]{4,3,1,2,0:T(4,128)(2,1)} %pad_maximum_fusion.1), calls=%async_computation.3 | async-start | bytes 65536 | tf_op jit(solution)/shard_map/all_to_all | solution.py:16
  204.0 10.8 %copy-start.1 = (bf16[320,512]{1,0:T(8,128)(2,1)S(1)}, bf16[320,512]{1,0:T(8,128)(2,1)}, u32[]{:S(2)}) copy-start(bf16[320,512]{1,0:T(8,128)(2,1)} %param.14) | copy-start | bytes 983044
  221.6 0.8 copy-start
  221.6 1.6 slice-start
  228.4 8.0 %collective-permute-start = (bf16[128,512]{1,0:T(8,128)(2,1)S(1)}, bf16[128,512]{1,0:T(8,128)(2,1)S(1)}, u32[]{:S(2)}, u32[]{:S(2)}) collective-permute-start(bf16[128,512]{1,0:T(8,128)(2,1)S(1)} %get-tuple-element.36), channel_id=1, source_target_pairs={{0,1},{1,2},{2,3},{3,4},{4,5},{5,6},{6,7},{7,8},{8,9},{9,10},{10,1... | collective-permute-start | bytes 393224 | tf_op jit(solution)/shard_map/ppermute | solution.py:26
  228.7 7.8 %collective-permute-start.1 = (bf16[128,512]{1,0:T(8,128)(2,1)S(1)}, bf16[128,512]{1,0:T(8,128)(2,1)S(1)}, u32[]{:S(2)}, u32[]{:S(2)}) collective-permute-start(bf16[128,512]{1,0:T(8,128)(2,1)S(1)} %get-tuple-element.37), channel_id=1, source_target_pairs={{1,0},{2,1},{3,2},{4,3},{5,4},{6,5},{7,6},{8,7},{9,8},{10,9},{11,1... | collective-permute-start | bytes 393224 | tf_op jit(solution)/shard_map/ppermute | solution.py:29
Sparse Core Ops, SparseCore 0:
  10.2 86.2 all-gather.2
